TPU v7x, 32 devices: a whole 2x2x4 slice. The times are simulated.
32 devices in a mesh: space: 8 (over y, x, core), mode: 4 (over z).
Axes of the slice: x: 2, y: 2, z: 4, core: 2. Of those that a mesh axis runs over, the one named last changes fastest.
Arguments:
- modes: bfloat16 [512, 96, 2048], P('mode', 'space'), may hold values from -6 to 6
- phases: int32 [96, 2048], P('space'), may hold values from 0 to 2
- velocity: float32 [3], replicated, may hold values from 0.5 to 1.5
Outputs:
- reduced: float32 [512, 512], P('space', 'mode')
All inputs are finite; a program needn't handle non-finite values.
Results may differ from a plain program's by a relative error of at most 0.0028.
Values may be sent and summed in bfloat16 or wider, within the bound.
No kernel may reach another device: no remote copies, remote signals or barrier semaphores. Data moves between devices by JAX's collectives and lax.ppermute only.
A program may use at most 192 MiB of HBM per device.

v0:
```python
import math
import jax
import jax.numpy as jnp
from jax import lax
from jax.sharding import PartitionSpec as P

NZ = 64


def extended(array, sides, width):
    for axis, dim in sides:
        devices, length = (lax.axis_size(axis), array.shape[dim])
        up = [(i, (i + 1) % devices) for i in range(devices - 1)]
        down = [(j, i) for i, j in up]
        last = lax.slice_in_dim(array, length - width, length, axis=dim)
        initial = lax.slice_in_dim(array, 0, width, axis=dim)
        before = lax.ppermute(last, axis, up)
        after = lax.ppermute(initial, axis, down)
        array = jnp.concatenate([before, array, after], axis=dim)
    return array


def shifted(field, offset):
    width = field.shape[-1]
    zeros_part = jnp.zeros(field.shape[:-1] + (abs(offset),), jnp.float32)
    if offset > 0:
        return jnp.concatenate([field[..., offset:], zeros_part], axis=-1)
    return jnp.concatenate([zeros_part, field[..., : width + offset]], axis=-1)


def inner_rows(left, right):
    left_flat = left.reshape(left.shape[0], -1)
    right_flat = right.reshape(right.shape[0], -1)
    return lax.dot_general(
        left_flat, right_flat, (((1,), (1,)), ((), ())), preferred_element_type=jnp.float32
    )


def local(modes, phases, velocity):
    weight = jnp.where(phases == 0, 0.1, jnp.where(phases == 1, 1.0, 0.5)).astype(jnp.float32)
    total_cells = lax.axis_size("space") * modes.shape[1] * modes.shape[2]
    eps = 1.0 / math.sqrt(total_cells)
    padded = extended(modes, (("space", 1),), 1).astype(jnp.float32)
    center = padded[:, 1:-1]
    x_up = padded[:, 2:]
    x_down = padded[:, :-2]
    zpos = lax.broadcasted_iota(jnp.int32, (1, 1, center.shape[-1]), 2) % NZ
    z_up = jnp.where(zpos == NZ - 1, 0.0, shifted(center, 1))
    z_down = jnp.where(zpos == 0, 0.0, shifted(center, -1))
    y_up = shifted(center, NZ)
    y_down = shifted(center, -NZ)
    spread = x_up + x_down + y_up + y_down + z_up + z_down - 6.0 * center
    drift = (
        velocity[0] * (x_up - x_down)
        + velocity[1] * (y_up - y_down)
        + velocity[2] * (z_up - z_down)
    )
    applied = (weight[None] * (eps * spread - 0.5 * drift)).astype(jnp.bfloat16)
    partial_cols = inner_rows(lax.all_gather(modes, "mode", axis=0, tiled=True), applied)
    summed = lax.psum_scatter(partial_cols, "space", scatter_dimension=0, tiled=True)
    return summed * eps


def solution(mesh):
    placed = (P("mode", "space", None), P("space", None), P())
    return jax.shard_map(
        local, mesh=mesh, in_specs=placed, out_specs=P("space", "mode"), check_vma=False
    )
```

profile of v0, /device:TPU:0, one launch (start us, length us, event | category | flops | bytes accessed | tf_op | source)
XLA Modules:
  0.0 492.9 jit_solution(3091800072277738935)
XLA Ops:
  6.5 0.0 all-gather.2.cloned.1.call-start
  6.5 0.7 all-gather.2.cloned.1.call-update
  7.3 0.0 reduce-scatter.4.cloned.1.call-start
  7.3 1.3 fusion.21
  8.6 2.4 collective-permute-start
  11.0 1.3 collective-permute-start.1
  12.3 1.4 fusion.22
  13.6 0.9 select_select_fusion
  14.6 0.0 collective-permute-done
  14.6 2.3 collective-permute-done.1
  16.9 12.4 %maximum_convert_fusion = f32[128,14,2048]{2,0,1:T(8,128)} fusion(bf16[128,1,2048]{2,0,1:T(8,128)(2,1)S(1)} %collective-permute-done.1, bf16[128,12,2048]{2,0,1:T(8,128)(2,1)} %param.3, bf16[128,1,2048]{2,0,1:T(8,128)(2,1)S(1)} %collective-permute-done), kind=kLoop, calls=%fused_computation.6 | loop fusion | flops 11010048 | bytes 22020096 | tf_op jit(solution)/shard_map/convert_element_type | solution.py:43
  29.2 0.0 copy-start
  29.2 22.5 %fusion.19 = (f32[128,12,1984]{2,0,1:T(8,128)}, f32[128,12,1984]{2,0,1:T(8,128)}) fusion(f32[128,14,2048]{2,0,1:T(8,128)} %maximum_convert_fusion), kind=kLoop, calls=%fused_computation.22 | loop fusion | bytes 48758784 | tf_op jit(solution)/shard_map/slice | solution.py:27
  51.7 0.0 copy-done
  51.7 10.0 %fusion.20 = (f32[128,12,2047]{2,0,1:T(8,128)}, f32[128,12,2047]{2,0,1:T(8,128)}) fusion(f32[128,14,2048]{2,0,1:T(8,128)S(1)} %copy-done), kind=kLoop, calls=%fused_computation.23 | loop fusion | bytes 50307072 | tf_op jit(solution)/shard_map/slice | solution.py:27
  61.8 34.4 %fusion.27 = bf16[128,12,2048]{2,0,1:T(8,128)(2,1)} fusion(f32[128,14,2048]{2,0,1:T(8,128)} %maximum_convert_fusion, f32[128,12,2047]{2,0,1:T(8,128)} %get-tuple-element.8, f32[128,12,2047]{2,0,1:T(8,128)} %get-tuple-element.7, f32[128,12,1984]{2,0,1:T(8,128)} %get-tuple-element.6, f32[128,12,1984]{2,0,1:T(8,128)} %get-tuple-element.5, ...), kind=kLoop, calls=%fused_computation.5.clone.clone.clone.clone.1 | loop fusion | flops 69206016 | bytes 93675536 | tf_op jit(solution)/shard_map/dot_general | solution.py:34
  96.2 340.7 %all-gather.2.cloned.1.call-done = bf16[512,12,2048]{2,0,1:T(8,128)(2,1)} async-done(((bf16[128,12,2048]{2,0,1:T(8,128)(2,1)}), bf16[512,12,2048]{2,0,1:T(8,128)(2,1)}) %all-gather.2.cloned.1.call-update) | async-done | bytes 25165840 | tf_op jit(solution)/shard_map/all_gather | solution.py:59
  436.8 15.1 %fusion.7 = f32[512,128]{0,1:T(8,128)S(1)} fusion(bf16[512,12,2048]{2,0,1:T(8,128)(2,1)} %all-gather.2.cloned.1.call-done, bf16[128,12,2048]{2,0,1:T(8,128)(2,1)} %fusion.27), kind=kOutput, calls=%fused_computation.8 | convolution fusion | flops 3221225472 | bytes 31719424 | tf_op jit(solution)/shard_map/dot_general | solution.py:34
  451.9 0.8 copy.7
  452.7 0.0 reduce-scatter.4.cloned.1.call-update
  452.8 32.0 %reduce-scatter.4.cloned.1.call-done = f32[64,128]{1,0:T(8,128)} async-done(((f32[512,128]{1,0:T(8,128)}), f32[64,128]{1,0:T(8,128)}) %reduce-scatter.4.cloned.1.call-update) | async-done | bytes 32784 | tf_op jit(solution)/shard_map/reduce_scatter | solution.py:60
  484.7 1.4 broadcast_multiply_fusion
  (1 shorter events, 0.0 us)
Async XLA Ops:
  6.5 430.3 %all-gather.2.cloned.1.call-start = ((), (), s32[]{:S(2)}) async-start(), calls=%async_computation.1 | async-start | bytes 31457280 | tf_op jit(solution)/shard_map/all_gather | solution.py:59
  7.3 477.5 %reduce-scatter.4.cloned.1.call-start = ((), (), s32[]{:S(2)}) async-start(), calls=%async_computation.2 | async-start | bytes 294912 | tf_op jit(solution)/shard_map/reduce_scatter | solution.py:60
  8.6 6.0 %collective-permute-start = (bf16[128,1,2048]{2,0,1:T(8,128)(2,1)S(1)}, bf16[128,1,2048]{2,0,1:T(8,128)(2,1)S(1)}, u32[]{:S(2)}, u32[]{:S(2)}) collective-permute-start(bf16[128,1,2048]{2,0,1:T(8,128)(2,1)S(1)} %get-tuple-element.9), channel_id=1, source_target_pairs={{0,4},{4,8},{8,12},{12,16},{16,20},{20,24},{24,28},{1,5},{5,9},{9,... | collective-permute-start | bytes 1572872 | tf_op jit(solution)/shard_map/ppermute | solution.py:17
  11.0 5.9 %collective-permute-start.1 = (bf16[128,1,2048]{2,0,1:T(8,128)(2,1)S(1)}, bf16[128,1,2048]{2,0,1:T(8,128)(2,1)S(1)}, u32[]{:S(2)}, u32[]{:S(2)}) collective-permute-start(bf16[128,1,2048]{2,0,1:T(8,128)(2,1)S(1)} %get-tuple-element.10), channel_id=1, source_target_pairs={{4,0},{8,4},{12,8},{16,12},{20,16},{24,20},{28,24},{5,1},{9,5},{13... | collective-permute-start | bytes 1572872 | tf_op jit(solution)/shard_map/ppermute | solution.py:18
  29.2 22.5 %copy-start = (f32[128,14,2048]{2,0,1:T(8,128)S(1)}, f32[128,14,2048]{2,0,1:T(8,128)}, u32[]{:S(2)}) copy-start(f32[128,14,2048]{2,0,1:T(8,128)} %maximum_convert_fusion) | copy-start | bytes 44040196
Sparse Core Ops, SparseCore 0:
  8.9 427.8 all-gather.1
  452.9 31.7 reduce-scatter.3
where the time goes:
time: 493 us
  waiting for transfers between devices  376 us (76%)
  other arithmetic  49.1 us (10%)
  local copies, waits for them, and re-layouts  36 us (7%)
  matrix products  15.1 us (3%)
  between operations  13.4 us (3%)
    all_gather x1, waiting for transfers between devices, local(): lax.all_gather(modes, 'mode', axis=0, tiled=True)  341 us
    dot_general x1, other arithmetic, inner_rows(): lax.dot_general(left_flat, right_flat, (((1,), (1,)), ((), ())), preferre...  34.4 us
    slice x2, local copies, waits for them, and re-layouts, shifted(): return jnp.concatenate([field[..., offset:], zeros_part], axis=-1)  32.5 us
    reduce_scatter x1, waiting for transfers between devices, local(): lax.psum_scatter(partial_cols, 'space', scatter_dimension=0, tiled=True)  32 us
    dot_general x1, matrix products, inner_rows(): lax.dot_general(left_flat, right_flat, (((1,), (1,)), ((), ())), preferre...  15.1 us
    convert_element_type x1, other arithmetic, local(): padded = extended(modes, (('space', 1),), 1).astype(jnp.float32)  12.4 us
  transfers between devices with their start and end apart: 4, of which 3 were waited for; matrix products, arithmetic and copies ran while one was open for 17% of the time, Pallas kernels for 0%

commit v1 on v0

--- a/solution.py
+++ b/solution.py
@@ -1,3 +1,4 @@
+import functools
 import math
 import jax
 import jax.numpy as jnp
@@ -5,6 +6,39 @@
 from jax.sharding import PartitionSpec as P
 
 NZ = 64
+
+
+def _manage_tails(sample, which_dim):
+    out_arr = list(sample.shape[1:])
+    out_arr[which_dim] *= sample.shape[0]
+    return jnp.moveaxis(sample, 0, which_dim).reshape(out_arr)
+
+
+def track_the_series_all(message, a_name, array_dim):
+    slots = []
+    extent = lax.axis_size(a_name)
+    for ii in range(extent):
+        slots.append((ii, (ii + 1) % extent))
+    nodes = []
+    for p, h in slots:
+        nodes.append((h, p))
+    base_arr, t_next = ([], [])
+    for ix in range(extent - 1):
+        if ix % 2 == 0:
+            next_value = lax.ppermute(base_arr[-1] if base_arr else message, a_name, slots)
+            base_arr.append(next_value)
+        else:
+            v1 = lax.ppermute(t_next[-1] if t_next else message, a_name, nodes)
+            t_next.append(v1)
+    r_now = jnp.stack([*base_arr[::-1], message, *t_next])
+    wide_out = lax.axis_index(a_name)
+    tall = len(base_arr)
+    current_value = wide_out - tall
+    r_now = r_now[(jnp.arange(extent) - current_value) % extent]
+    return _manage_tails(r_now, array_dim)
+
+
+field_step_on = functools.partial(track_the_series_all, a_name="mode", array_dim=0)
 
 
 def extended(array, sides, width):
@@ -56,7 +90,7 @@
         + velocity[2] * (z_up - z_down)
     )
     applied = (weight[None] * (eps * spread - 0.5 * drift)).astype(jnp.bfloat16)
-    partial_cols = inner_rows(lax.all_gather(modes, "mode", axis=0, tiled=True), applied)
+    partial_cols = inner_rows(field_step_on(modes), applied)
     summed = lax.psum_scatter(partial_cols, "space", scatter_dimension=0, tiled=True)
     return summed * eps
 

time: 493 us -> 596 us (1.21)
  local copies, waits for them, and re-layouts: 36 us -> 123 us
  other arithmetic: 49.1 us -> 70.7 us
  waiting for transfers between devices: 376 us -> 363 us
    all_gather x1 -> x0, waiting for transfers between devices: 341 us -> none  [local(): lax.all_gather(modes, 'mode', axis=0, tiled=True)]
    ppermute x0 -> x3, waiting for transfers between devices: none -> 329 us  [the longest x2 258 us: track_the_series_all(): lax.ppermute(base_arr[-1] if base_arr else message, a_name, slots)]
    unnamed x3 -> x12, local copies, waits for them, and re-layouts: 0.84 us -> 47.4 us
    gather x0 -> x5, local copies, waits for them, and re-layouts: none -> 44.3 us  [track_the_series_all(): r_now = r_now[(jnp.arange(extent) - current_value) % extent]]
    dot_general x1 -> x0, other arithmetic: 34.4 us -> none  [inner_rows(): lax.dot_general(left_flat, right_flat, (((1,), (1,)), ((), ())), preferre...]
    convert_element_type x0 -> x1, other arithmetic: none -> 23.8 us  [local(): applied = (weight[None] * (eps * spread - 0.5 * drift)).astype(jnp.bfloat16)]
    another operation x0 -> x1, other arithmetic: none -> 18.2 us  [track_the_series_all(): r_now = jnp.stack([*base_arr[::-1], message, *t_next])]
    unnamed x0 -> x2, other arithmetic: none -> 17.4 us
  transfers between devices with their start and end apart: 4 -> 6, of which waited for: 3 -> 4; matrix products, arithmetic and copies ran while one was open for 17% -> 12% of each run, Pallas kernels for 0% -> 0%
where the time goes in v1:
time: 596 us; the launch traced here: 595 us
  waiting for transfers between devices  363 us (61%)
  local copies, waits for them, and re-layouts  123 us (21%)
  other arithmetic  70.7 us (12%)
  matrix products  17.3 us (3%)
  between operations  13.5 us (2%)
  starting transfers between devices  7.9 us (1%)
    ppermute x2, waiting for transfers between devices, track_the_series_all(): lax.ppermute(base_arr[-1] if base_arr else message, a_name, slots)  258 us
    ppermute x1, waiting for transfers between devices, track_the_series_all(): v1 = lax.ppermute(t_next[-1] if t_next else message, a_name, nodes)  71 us
    unnamed x12, local copies, waits for them, and re-layouts  47.4 us
    gather x5, local copies, waits for them, and re-layouts, track_the_series_all(): r_now = r_now[(jnp.arange(extent) - current_value) % extent]  44.3 us
    reduce_scatter x1, waiting for transfers between devices, local(): lax.psum_scatter(partial_cols, 'space', scatter_dimension=0, tiled=True)  33.1 us
    slice x2, local copies, waits for them, and re-layouts, shifted(): return jnp.concatenate([field[..., offset:], zeros_part], axis=-1)  28.9 us
    convert_element_type x1, other arithmetic, local(): applied = (weight[None] * (eps * spread - 0.5 * drift)).astype(jnp.bfloat16)  23.8 us
    another operation x1, other arithmetic, track_the_series_all(): r_now = jnp.stack([*base_arr[::-1], message, *t_next])  18.2 us
  transfers between devices with their start and end apart: 6, of which 4 were waited for; matrix products, arithmetic and copies ran while one was open for 12% of the time, Pallas kernels for 0%

profile of v1, /device:TPU:0, one launch (start us, length us, event | category | flops | bytes accessed | tf_op | source)
XLA Modules:
  0.0 594.5 jit_solution(15472242460411354814)
XLA Ops:
  6.5 0.0 reduce-scatter.2.cloned.1.call-start
  6.5 3.0 collective-permute-start
  9.6 2.1 collective-permute-start.2
  11.6 8.6 %copy.5 = bf16[128,12,2048]{0,2,1:T(8,128)(2,1)} copy(bf16[128,12,2048]{2,0,1:T(8,128)(2,1)} %param.3) | data formatting | bytes 12582912 | tf_op args[0]
  20.3 1.3 fusion.18
  21.5 1.5 collective-permute-start.3
  23.0 1.3 collective-permute-start.4
  24.4 0.0 copy-done.2
  24.4 0.6 fusion.19
  25.0 123.3 %collective-permute-done = bf16[128,12,2048]{2,0,1:T(8,128)(2,1)} collective-permute-done((bf16[128,12,2048]{2,0,1:T(8,128)(2,1)}, bf16[128,12,2048]{2,0,1:T(8,128)(2,1)}, u32[]{:S(2)}, u32[]{:S(2)}) %collective-permute-start) | collective-permute-done | bytes 6291488 | tf_op jit(solution)/shard_map/ppermute | solution.py:28
  148.3 0.0 collective-permute-start.1
  148.3 0.7 select_select_fusion
  149.0 0.0 collective-permute-done.3
  149.0 0.0 collective-permute-done.4
  149.0 9.2 %maximum_convert_fusion = f32[128,14,2048]{0,2,1:T(8,128)} fusion(bf16[128,1,2048]{0,2,1:T(8,128)(2,1)S(1)} %collective-permute-done.4, bf16[128,12,2048]{0,2,1:T(8,128)(2,1)} %copy.5, bf16[128,1,2048]{0,2,1:T(8,128)(2,1)S(1)} %collective-permute-done.3), kind=kLoop, calls=%fused_computation.15 | loop fusion | flops 11010048 | bytes 22020096 | tf_op jit(solution)/shard_map/convert_element_type | solution.py:77
  158.1 20.0 %fusion.17 = (f32[128,12,2047]{0,2,1:T(8,128)}, f32[128,12,2047]{0,2,1:T(8,128)}) fusion(f32[128,14,2048]{0,2,1:T(8,128)} %maximum_convert_fusion), kind=kLoop, calls=%fused_computation.34 | loop fusion | bytes 50307072 | tf_op jit(solution)/shard_map/slice | solution.py:61
  178.1 9.0 %fusion.16 = (f32[128,12,1984]{0,2,1:T(8,128)}, f32[128,12,1984]{0,2,1:T(8,128)}) fusion(f32[128,14,2048]{0,2,1:T(8,128)S(1)} %copy-done), kind=kLoop, calls=%fused_computation.33 | loop fusion | bytes 48758784 | tf_op jit(solution)/shard_map/slice | solution.py:61
  187.1 23.8 %fusion.7 = bf16[128,12,2048]{0,2,1:T(8,128)(2,1)} fusion(f32[128,14,2048]{0,2,1:T(8,128)S(1)} %copy-done, f32[128,12,2047]{0,2,1:T(8,128)} %get-tuple-element.12, f32[128,12,2047]{0,2,1:T(8,128)} %get-tuple-element.11, f32[128,12,1984]{0,2,1:T(8,128)} %get-tuple-element.10, f32[128,12,1984]{0,2,1:T(8,128)} %get-tuple-element.9, f32[]{:T(128)} %bitcast.7, ...), kind=kLoop, calls=%fused_computation.14 | loop fusion | flops 69206016 | bytes 93675536 | tf_op jit(solution)/shard_map/convert_element_type | solution.py:92
  210.9 71.0 %collective-permute-done.2 = bf16[128,12,2048]{2,0,1:T(8,128)(2,1)} collective-permute-done((bf16[128,12,2048]{2,0,1:T(8,128)(2,1)}, bf16[128,12,2048]{2,0,1:T(8,128)(2,1)}, u32[]{:S(2)}, u32[]{:S(2)}) %collective-permute-start.2) | collective-permute-done | bytes 6291488 | tf_op jit(solution)/shard_map/ppermute | solution.py:31
  281.9 135.2 %collective-permute-done.1 = bf16[128,12,2048]{2,0,1:T(8,128)(2,1)} collective-permute-done((bf16[128,12,2048]{2,0,1:T(8,128)(2,1)}, bf16[128,12,2048]{2,0,1:T(8,128)(2,1)}, u32[]{:S(2)}, u32[]{:S(2)}) %collective-permute-start.1) | collective-permute-done | bytes 6291488 | tf_op jit(solution)/shard_map/ppermute | solution.py:28
  417.1 18.2 %pad_maximum_fusion = bf16[4,128,12,2048]{3,1,2,0:T(8,128)(2,1)} fusion(bf16[1,128,12,2048]{3,1,2,0:T(8,128)(2,1)} %bitcast.3, bf16[1,128,12,2048]{3,1,2,0:T(8,128)(2,1)S(1)} %bitcast.21, bf16[1,128,12,2048]{3,1,2,0:T(8,128)(2,1)} %bitcast.1, bf16[1,128,12,2048]{3,1,2,0:T(8,128)(2,1)} %bitcast), kind=kLoop, calls=%fused_computation.7 | loop fusion | flops 37748736 | bytes 50331648 | tf_op jit(solution)/shard_map/stack | solution.py:33
  435.3 18.7 %fusion.15 = (bf16[4,128,12,512]{3,1,2,0:T(8,128)(2,1)}, bf16[4,128,12,512]{3,1,2,0:T(8,128)(2,1)}, bf16[4,128,12,512]{3,1,2,0:T(8,128)(2,1)}, bf16[4,128,12,512]{3,1,2,0:T(8,128)(2,1)}) fusion(bf16[4,128,12,2048]{3,1,2,0:T(8,128)(2,1)} %pad_maximum_fusion), kind=kLoop, calls=%fused_computation.32 | loop fusion | bytes 50331648 | tf_op jit(solution)/shard_map/gather | solution.py:37
  454.0 6.3 %gather_fusion = bf16[4,128,12,512]{3,1,2,0:T(8,128)(2,1)} fusion(bf16[4,128,12,512]{3,1,2,0:T(8,128)(2,1)} %get-tuple-element.5, s32[1024]{0:T(1024)S(1)} %pad_clamp_fusion), kind=kCustom, calls=%fused_computation | custom fusion | bytes 12582928 | tf_op jit(solution)/shard_map/gather | solution.py:37
  460.4 6.4 %gather_fusion.1 = bf16[4,128,12,512]{3,1,2,0:T(8,128)(2,1)} fusion(bf16[4,128,12,512]{3,1,2,0:T(8,128)(2,1)} %get-tuple-element.7, s32[1024]{0:T(1024)S(1)} %pad_clamp_fusion), kind=kCustom, calls=%fused_computation.1 | custom fusion | bytes 12582928 | tf_op jit(solution)/shard_map/gather | solution.py:37
  466.8 6.5 %gather_fusion.2 = bf16[4,128,12,512]{3,1,2,0:T(8,128)(2,1)} fusion(bf16[4,128,12,512]{3,1,2,0:T(8,128)(2,1)} %get-tuple-element.6, s32[1024]{0:T(1024)S(1)} %pad_clamp_fusion), kind=kCustom, calls=%fused_computation.2 | custom fusion | bytes 12582928 | tf_op jit(solution)/shard_map/gather | solution.py:37
  473.3 6.3 %gather_fusion.3 = bf16[4,128,12,512]{3,1,2,0:T(8,128)(2,1)} fusion(bf16[4,128,12,512]{3,1,2,0:T(8,128)(2,1)} %get-tuple-element.8, s32[1024]{0:T(1024)S(1)} %pad_clamp_fusion), kind=kCustom, calls=%fused_computation.3 | custom fusion | bytes 12582928 | tf_op jit(solution)/shard_map/gather | solution.py:37
  479.6 17.4 %pad_maximum_fusion.1 = bf16[4,128,12,2048]{3,1,2,0:T(8,128)(2,1)} fusion(bf16[4,128,12,512]{3,1,2,0:T(8,128)(2,1)} %gather_fusion.3, bf16[4,128,12,512]{3,1,2,0:T(8,128)(2,1)} %gather_fusion.2, bf16[4,128,12,512]{3,1,2,0:T(8,128)(2,1)} %gather_fusion.1, bf16[4,128,12,512]{3,1,2,0:T(8,128)(2,1)} %gather_fusion), kind=kLoop, calls=%fused_computation.8 | loop fusion | flops 100663296 | bytes 50331648
  497.1 38.8 %copy.4 = bf16[4,128,12,2048]{1,0,3,2:T(4,128)(2,1)} copy(bf16[4,128,12,2048]{3,1,2,0:T(8,128)(2,1)} %pad_maximum_fusion.1) | data formatting | bytes 50331648
  535.8 17.3 %fusion = f32[512,128]{1,0:T(8,128)} fusion(bf16[128,24576]{0,1:T(8,128)(2,1)} %bitcast.22, bf16[3072,8,4,128]{3,2,1,0:T(4,128)(2,1)} %bitcast.18), kind=kOutput, calls=%fused_computation.4 | convolution fusion | flops 3221225472 | bytes 31719424 | tf_op jit(solution)/shard_map/dot_general | solution.py:68
  553.2 0.0 reduce-scatter.2.cloned.1.call-update
  553.2 33.1 %reduce-scatter.2.cloned.1.call-done = f32[64,128]{1,0:T(8,128)} async-done(((f32[512,128]{1,0:T(8,128)}), f32[64,128]{1,0:T(8,128)}) %reduce-scatter.2.cloned.1.call-update) | async-done | bytes 32784 | tf_op jit(solution)/shard_map/reduce_scatter | solution.py:94
  586.3 1.4 broadcast_multiply_fusion
  (13 shorter events, 0.0 us)
Async XLA Ops:
  6.5 17.8 %copy-start.2 = (f32[3]{0:T(128)S(1)}, f32[3]{0:T(128)}, u32[]{:S(2)}) copy-start(f32[3]{0:T(128)} %param.5) | copy-start | bytes 40
  6.5 141.8 %copy-start.1 = (s32[12,2048]{1,0:T(8,128)S(1)}, s32[12,2048]{1,0:T(8,128)}, u32[]{:S(2)}) copy-start(s32[12,2048]{1,0:T(8,128)} %param.4) | copy-start | bytes 294916
  6.5 579.7 %reduce-scatter.2.cloned.1.call-start = ((), (), s32[]{:S(2)}) async-start(), calls=%async_computation.1 | async-start | bytes 294912 | tf_op jit(solution)/shard_map/reduce_scatter | solution.py:94
  6.5 141.8 %collective-permute-start = (bf16[128,12,2048]{2,0,1:T(8,128)(2,1)}, bf16[128,12,2048]{2,0,1:T(8,128)(2,1)}, u32[]{:S(2)}, u32[]{:S(2)}) collective-permute-start(bf16[128,12,2048]{2,0,1:T(8,128)(2,1)} %param.3), channel_id=1, source_target_pairs={{0,1},{1,2},{2,3},{3,0},{4,5},{5,6},{6,7},{7,4},{8,9},{9,10},{10,1... | collective-permute-start | bytes 18874376 | tf_op jit(solution)/shard_map/ppermute | solution.py:28
  9.6 272.3 %collective-permute-start.2 = (bf16[128,12,2048]{2,0,1:T(8,128)(2,1)}, bf16[128,12,2048]{2,0,1:T(8,128)(2,1)}, u32[]{:S(2)}, u32[]{:S(2)}) collective-permute-start(bf16[128,12,2048]{2,0,1:T(8,128)(2,1)} %param.3), channel_id=1, source_target_pairs={{1,0},{2,1},{3,2},{0,3},{5,4},{6,5},{7,6},{4,7},{9,8},{10,9},{11,1... | collective-permute-start | bytes 18874376 | tf_op jit(solution)/shard_map/ppermute | solution.py:31
  21.5 127.4 %collective-permute-start.3 = (bf16[128,1,2048]{0,2,1:T(8,128)(2,1)S(1)}, bf16[128,1,2048]{0,2,1:T(8,128)(2,1)S(1)}, u32[]{:S(2)}, u32[]{:S(2)}) collective-permute-start(bf16[128,1,2048]{0,2,1:T(8,128)(2,1)S(1)} %get-tuple-element.13), channel_id=1, source_target_pairs={{0,4},{4,8},{8,12},{12,16},{16,20},{20,24},{24,28},{1,5},{5,9},{9,... | collective-permute-start | bytes 1572872 | tf_op jit(solution)/shard_map/ppermute | solution.py:51
  23.0 125.9 %collective-permute-start.4 = (bf16[128,1,2048]{0,2,1:T(8,128)(2,1)S(1)}, bf16[128,1,2048]{0,2,1:T(8,128)(2,1)S(1)}, u32[]{:S(2)}, u32[]{:S(2)}) collective-permute-start(bf16[128,1,2048]{0,2,1:T(8,128)(2,1)S(1)} %get-tuple-element.14), channel_id=1, source_target_pairs={{4,0},{8,4},{12,8},{16,12},{20,16},{24,20},{28,24},{5,1},{9,5},{13... | collective-permute-start | bytes 1572872 | tf_op jit(solution)/shard_map/ppermute | solution.py:52
  148.3 268.8 %collective-permute-start.1 = (bf16[128,12,2048]{2,0,1:T(8,128)(2,1)}, bf16[128,12,2048]{2,0,1:T(8,128)(2,1)}, u32[]{:S(2)}, u32[]{:S(2)}) collective-permute-start(bf16[128,12,2048]{2,0,1:T(8,128)(2,1)} %collective-permute-done), channel_id=1, source_target_pairs={{0,1},{1,2},{2,3},{3,0},{4,5},{5,6},{6,7},{7,4},{8,9},{9,10},{10,1... | collective-permute-start | bytes 18874376 | tf_op jit(solution)/shard_map/ppermute | solution.py:28
  158.1 20.0 %copy-start = (f32[128,14,2048]{0,2,1:T(8,128)S(1)}, f32[128,14,2048]{0,2,1:T(8,128)}, u32[]{:S(2)}) copy-start(f32[128,14,2048]{0,2,1:T(8,128)} %maximum_convert_fusion) | copy-start | bytes 44040196
  178.1 239.0 %slice-start = ((s8[6291456]{0:T(1024)(128)(4,1)}), s8[4194304]{0:T(1024)(128)(4,1)S(1)}, s32[]{:S(2)}) async-start(s8[6291456]{0:T(1024)(128)(4,1)} %bitcast.19), calls=%async_computation.2 | async-start | bytes 8388608
  187.1 230.0 %slice-start.1 = ((s8[6291456]{0:T(1024)(128)(4,1)}), s8[2097152]{0:T(1024)(128)(4,1)S(1)}, s32[]{:S(2)}) async-start(s8[6291456]{0:T(1024)(128)(4,1)} %bitcast.19), calls=%async_computation.3 | async-start | bytes 4194304
Sparse Core Ops, SparseCore 0:
  553.3 32.9 reduce-scatter.1
